TPU v7x, 32 devices: a whole 2x2x4 slice. The times are simulated.
32 devices in a mesh: ab: 2 (over y), cd: 16 (over z, x, core).
Axes of the slice: x: 2, y: 2, z: 4, core: 2. Of those that a mesh axis runs over, the one named last changes fastest.
Arguments:
- amplitudes: float32 [768, 16384], P('cd', 'ab'), may hold values from -1.25 to 1.25
- driver: float32 [768, 16384], P('cd', 'ab'), may hold values from -6 to 6
- ladder: bfloat16 [16384, 16384], P('ab', 'cd'), may hold values from -0.125 to 0.125
- block_mask: int32 [128, 128], P('ab', 'cd'), may hold values 0 or 1
- pair_list: int32 [768], replicated, may hold values from 0 to 1023, as said below
- occ_energy: float32 [32], replicated, may hold values from -2 to -0.5
- virt_energy: float32 [128], replicated, may hold values from 0.5 to 3
Outputs:
- new_amplitudes: float32 [768, 16384], P('cd', 'ab')
Inputs may be any that keep to these rules, and one draw needn't show every extreme that they name: `pair_list`: the entries are distinct occupied pairs i * 32 + j. Rows come in aligned blocks of two: a pair with i != j shares its block with the pair (j, i); pairs with i == j stand two to a block. Pairs 0 and 1023 are always listed.
All inputs are finite; a program needn't handle non-finite values. No bound on the sum of `block_mask` on one device may be relied on, other than what follows from the above.
Results may differ from a plain program's by a relative error of at most 0.008.
Values may be sent and summed in bfloat16 or wider, within the bound.
A program may use at most 128 MiB of HBM per device.

v0:
```python
import jax
import jax.numpy as jnp
from jax import lax
from jax.sharding import PartitionSpec as P

NV = 128
NOCC = 32
BLK = 128
ITERS = 2


def swap_rows(values, diagonal_rows):
    row_count = values.shape[0]
    swapped = jnp.flip(values.reshape(row_count // 2, 2, -1), axis=1).reshape(row_count, -1)
    return jnp.where(diagonal_rows[:, None], values, swapped)


def flip_pairs(tiles, diagonal_rows, tile_width):
    row_count = tiles.shape[0]
    tile_count = tiles.shape[1]
    turned = jnp.swapaxes(tiles.reshape(row_count, tile_count, tile_width, tile_width), 2, 3)
    turned = turned.reshape(row_count, tile_count * tile_width * tile_width)
    return swap_rows(turned, diagonal_rows)


def body(amplitudes, driver, ladder, block_mask, pair_list, occ_energy, virt_energy):
    ab_count = lax.axis_size("ab")
    ab_index = lax.axis_index("ab")
    cd_index = lax.axis_index("cd")
    rows_dev, cols_dev = amplitudes.shape
    out_rows, in_cols = ladder.shape
    tile_width = NV // ab_count
    tile_area = tile_width * tile_width
    weights = ladder.reshape(out_rows // BLK, BLK, in_cols // BLK, BLK)
    weights = (weights * block_mask.astype(jnp.bfloat16)[:, None, :, None]).reshape(
        out_rows, in_cols
    )
    pairs_local = ab_index * cols_dev + jnp.arange(cols_dev, dtype=jnp.int32)
    big_a = pairs_local // (tile_width * NV)
    big_b = pairs_local // tile_area % ab_count
    first = big_a * tile_width + pairs_local // tile_width % tile_width
    second = big_b * tile_width + pairs_local % tile_width
    virt_index = jnp.arange(NV, dtype=jnp.int32)
    picks = (first[:, None] == virt_index).astype(jnp.float32) + (
        second[:, None] == virt_index
    ).astype(jnp.float32)
    col_energy = jnp.dot(picks, virt_energy, precision=lax.Precision.HIGHEST)
    row_pairs = lax.dynamic_slice_in_dim(pair_list, cd_index * rows_dev, rows_dev)
    occ_index = jnp.arange(NOCC, dtype=jnp.int32)
    occ_picks = (row_pairs[:, None] // NOCC == occ_index).astype(jnp.float32)
    occ_picks = occ_picks + (row_pairs[:, None] % NOCC == occ_index).astype(jnp.float32)
    row_energy = jnp.dot(occ_picks, occ_energy, precision=lax.Precision.HIGHEST)
    denominator = col_energy[None, :] - row_energy[:, None]
    local_diagonal = row_pairs // NOCC == row_pairs % NOCC
    turned_weights = jnp.swapaxes(
        weights.reshape(out_rows // tile_area, tile_width, tile_width, in_cols), 1, 2
    )
    turned_weights = turned_weights.reshape(out_rows, in_cols)
    state = amplitudes
    for step in range(ITERS):
        rounded = state.astype(jnp.bfloat16)
        regrouped = lax.all_to_all(rounded, "cd", split_axis=1, concat_axis=0, tiled=True)
        partial_value = lax.dot_general(
            lax.all_gather(regrouped, "ab", axis=1, tiled=True),
            weights,
            (((1,), (1,)), ((), ())),
            preferred_element_type=jnp.float32,
        )
        total = lax.psum_scatter(
            partial_value.astype(jnp.bfloat16), "cd", scatter_dimension=0, tiled=True
        ).astype(jnp.float32)
        tiles = lax.all_to_all(
            total.reshape(rows_dev, ab_count, tile_area).astype(jnp.bfloat16),
            "ab",
            split_axis=1,
            concat_axis=1,
            tiled=True,
        ).astype(jnp.float32)
        symmetric = total + flip_pairs(tiles, local_diagonal, tile_width)
        state = (driver + symmetric) / denominator
    return state


def solution(mesh):
    placed = (P("cd", "ab"), P("cd", "ab"), P("ab", "cd"), P("ab", "cd"), P(), P(), P())
    return jax.shard_map(body, mesh=mesh, in_specs=placed, out_specs=P("cd", "ab"), check_vma=False)
```

profile of v0, /device:TPU:0, one launch (start us, length us, event | category | flops | bytes accessed | tf_op | source)
XLA Modules:
  0.0 568.7 jit_solution(2987417950333544323)
XLA Ops:
  6.5 0.0 copy-start
  6.5 0.0 all-gather.3.cloned.1.call-start
  6.5 1.5 convert_element_type.47
  8.0 0.1 copy.77
  8.1 0.0 copy-start.2
  8.1 27.4 %all_to_all.48 = bf16[48,16,512]{2,0,1:T(8,128)(2,1)} all-to-all(bf16[48,16,512]{2,0,1:T(8,128)(2,1)S(1)} %bitcast.59), channel_id=1, replica_groups=mesh['ab'=2,'cd'=16] {'cd'}, dimensions={1} | all-to-all | bytes 1572864 | tf_op jit(solution)/shard_map/all_to_all | solution.py:62
  35.5 0.0 all-gather.3.cloned.1.call-update
  35.6 0.0 reduce-scatter.7.cloned.1.call-start
  35.6 0.0 copy-done.2
  35.6 0.1 copy.52
  35.7 26.5 %all-gather.3.cloned.1.call-done = bf16[768,1024]{1,0:T(8,128)(2,1)} async-done(((bf16[768,512]{1,0:T(8,128)(2,1)}), bf16[768,1024]{1,0:T(8,128)(2,1)}) %all-gather.3.cloned.1.call-update) | async-done | bytes 1572880 | tf_op jit(solution)/shard_map/all_gather | solution.py:64
  62.2 0.0 copy-start.3
  62.2 6.1 %mul.31 = bf16[64,128,8,128]{3,2,1,0:T(8,128)(2,1)} broadcast(bf16[64,8]{1,0:T(8,128)(2,1)S(1)} %copy.52), dimensions={0,2} | broadcast | bytes 16778240 | tf_op jit(solution)/shard_map/mul | solution.py:35
  68.3 0.0 copy-done.3
  68.3 22.4 %fusion = bf16[768,8192]{0,1:T(8,128)(2,1)} fusion(bf16[768,1024]{1,0:T(8,128)(2,1)S(1)} %copy-done.3, bf16[8192,1024]{1,0:T(8,128)(2,1)} %param.9, bf16[1024,8,8,128]{3,2,1,0:T(8,128)(2,1)} %bitcast.51), kind=kOutput, calls=%fused_computation.3 | convolution fusion | flops 12899581952 | bytes 47710208 | tf_op jit(solution)/shard_map/dot_general | solution.py:63
  90.7 16.7 %copy.64 = bf16[768,8192]{1,0:T(8,128)(2,1)} copy(bf16[768,8192]{0,1:T(8,128)(2,1)} %fusion) | data formatting | bytes 25165824
  107.4 0.0 reduce-scatter.7.cloned.1.call-update
  107.4 0.1 fusion.10
  107.5 135.0 %reduce-scatter.7.cloned.1.call-done = bf16[48,8192]{1,0:T(8,128)(2,1)} async-done(((bf16[768,8192]{1,0:T(8,128)(2,1)}), bf16[48,8192]{1,0:T(8,128)(2,1)}) %reduce-scatter.7.cloned.1.call-update) | async-done | bytes 786448 | tf_op jit(solution)/shard_map/reduce_scatter | solution.py:69
  242.5 2.0 copy.65
  244.4 0.0 copy-start.4
  244.5 1.6 copy.55
  246.0 3.5 all-to-all-start.1
  249.6 0.0 all-gather.5.cloned.1.call-start
  249.6 0.8 fusion.29
  250.4 0.0 copy-done.4
  250.4 0.2 convolution_bitcast_fusion
  250.6 0.0 copy-done
  250.6 6.4 %fusion.1 = f32[1,8192]{1,0:T(1,128)S(1)} fusion(s32[8192]{0:T(1024)S(1)} %get-tuple-element.9, s32[8192]{0:T(1024)S(1)} %get-tuple-element.8, f32[128]{0:T(128)S(1)} %copy-done), kind=kOutput, calls=%fused_computation.4 | convolution fusion | flops 17825792 | bytes 98816 | tf_op jit(solution)/shard_map/dot_general | solution.py:47
  257.0 2.8 all-to-all-done.1
  259.8 2.4 reshape.147
  262.2 2.4 copy.56
  264.6 1.9 reshape.142
  266.5 2.5 reshape_reshape.6
  269.0 26.0 %rev.7 = f32[24,2,8192]{2,1,0:T(2,128)S(1)} reverse(f32[24,2,8192]{2,1,0:T(2,128)} %reshape_reshape.6), dimensions={1} | reverse | bytes 3145728 | tf_op jit(solution)/shard_map/jit(_flip)/rev | solution.py:14
  295.0 1.1 reshape.143
  296.1 2.7 fusion.7
  298.8 0.1 copy.76
  298.9 25.1 %all_to_all.49 = bf16[48,16,512]{2,0,1:T(8,128)(2,1)} all-to-all(bf16[48,16,512]{2,0,1:T(8,128)(2,1)S(1)} %bitcast.60), channel_id=1, replica_groups=mesh['ab'=2,'cd'=16] {'cd'}, dimensions={1} | all-to-all | bytes 1572864 | tf_op jit(solution)/shard_map/all_to_all | solution.py:62
  324.0 0.0 all-gather.5.cloned.1.call-update
  324.0 0.0 reduce-scatter.9.cloned.1.call-start
  324.1 25.6 %all-gather.5.cloned.1.call-done = bf16[768,1024]{1,0:T(8,128)(2,1)} async-done(((bf16[768,512]{1,0:T(8,128)(2,1)}), bf16[768,1024]{1,0:T(8,128)(2,1)}) %all-gather.5.cloned.1.call-update) | async-done | bytes 1572880 | tf_op jit(solution)/shard_map/all_gather | solution.py:64
  349.7 21.7 %convolution_convert_fusion = bf16[768,8192]{1,0:T(8,128)(2,1)} fusion(bf16[768,1024]{1,0:T(8,128)(2,1)} %all-gather.5.cloned.1.call-done, bf16[8192,1024]{1,0:T(8,128)(2,1)} %param.9, bf16[1024,8,8,128]{3,2,1,0:T(8,128)(2,1)} %bitcast.52), kind=kOutput, calls=%fused_computation.1 | convolution fusion | flops 12899581952 | bytes 47710208 | tf_op jit(solution)/shard_map/dot_general | solution.py:63
  371.4 0.0 reduce-scatter.9.cloned.1.call-update
  371.5 135.0 %reduce-scatter.9.cloned.1.call-done = bf16[48,8192]{1,0:T(8,128)(2,1)} async-done(((bf16[768,8192]{1,0:T(8,128)(2,1)}), bf16[48,8192]{1,0:T(8,128)(2,1)}) %reduce-scatter.9.cloned.1.call-update) | async-done | bytes 786448 | tf_op jit(solution)/shard_map/reduce_scatter | solution.py:69
  506.5 2.0 copy.67
  508.5 0.8 copy.61
  509.3 12.7 %all_to_all.50 = bf16[48,2,4096]{2,0,1:T(8,128)(2,1)S(1)} all-to-all(bf16[48,2,4096]{2,0,1:T(8,128)(2,1)S(1)} %copy.61), channel_id=1, replica_groups=mesh['ab'=2,'cd'=16] {'ab'}, dimensions={1} | all-to-all | bytes 1572864 | tf_op jit(solution)/shard_map/all_to_all | solution.py:72
  522.1 2.4 reshape.148
  524.4 2.4 copy.62
  526.8 1.9 reshape.145
  528.7 2.5 reshape_reshape.7
  531.3 26.0 %rev.8 = f32[24,2,8192]{2,1,0:T(2,128)S(1)} reverse(f32[24,2,8192]{2,1,0:T(2,128)} %reshape_reshape.7), dimensions={1} | reverse | bytes 3145728 | tf_op jit(solution)/shard_map/jit(_flip)/rev | solution.py:14
  557.3 1.1 reshape.146
  558.3 0.0 copy-start.1
  558.4 3.8 subtract_divide_fusion
  562.2 0.0 copy-done.1
  (1 shorter events, 0.0 us)
Async XLA Ops:
  6.5 244.1 %copy-start = (f32[128]{0:T(128)S(1)}, f32[128]{0:T(128)}, u32[]{:S(2)}) copy-start(f32[128]{0:T(128)} %param.13) | copy-start | bytes 1540
  6.5 55.7 %all-gather.3.cloned.1.call-start = ((), (), s32[]{:S(2)}) async-start(), calls=%async_computation.6 | async-start | bytes 2359296 | tf_op jit(solution)/shard_map/all_gather | solution.py:64
  8.1 27.5 %copy-start.2 = (s32[64,8]{0,1:T(8,128)S(1)}, s32[64,8]{0,1:T(8,128)}, u32[]{:S(2)}) copy-start(s32[64,8]{0,1:T(8,128)} %param.10) | copy-start | bytes 6148
  35.6 206.9 %reduce-scatter.7.cloned.1.call-start = ((), (), s32[]{:S(2)}) async-start(), calls=%async_computation.8 | async-start | bytes 13369344 | tf_op jit(solution)/shard_map/reduce_scatter | solution.py:69
  62.2 6.1 %copy-start.3 = (bf16[768,1024]{1,0:T(8,128)(2,1)S(1)}, bf16[768,1024]{1,0:T(8,128)(2,1)}, u32[]{:S(2)}) copy-start(bf16[768,1024]{1,0:T(8,128)(2,1)} %all-gather.3.cloned.1.call-done) | copy-start | bytes 4718596
  244.4 5.9 %copy-start.4 = (f32[32]{0:T(128)S(1)}, f32[32]{0:T(128)}, u32[]{:S(2)}) copy-start(f32[32]{0:T(128)} %param.12) | copy-start | bytes 388
  246.0 13.8 %all-to-all-start.1 = ((bf16[48,2,4096]{2,0,1:T(8,128)(2,1)}), bf16[48,2,4096]{2,0,1:T(8,128)(2,1)S(1)}, u32[]{:S(2)}, u32[]{:S(2)}) async-start(bf16[48,2,4096]{2,0,1:T(8,128)(2,1)} %copy.55), calls=%async_computation.1 | async-start | bytes 1572864 | tf_op jit(solution)/shard_map/all_to_all | solution.py:72
  249.6 100.2 %all-gather.5.cloned.1.call-start = ((), (), s32[]{:S(2)}) async-start(), calls=%async_computation.7 | async-start | bytes 2359296 | tf_op jit(solution)/shard_map/all_gather | solution.py:64
  324.0 182.5 %reduce-scatter.9.cloned.1.call-start = ((), (), s32[]{:S(2)}) async-start(), calls=%async_computation.9 | async-start | bytes 13369344 | tf_op jit(solution)/shard_map/reduce_scatter | solution.py:69
  558.3 3.8 copy-start.1
Sparse Core Ops, SparseCore 0:
  35.7 26.4 all-gather.2
  107.5 134.9 reduce-scatter.6
  324.2 25.5 all-gather.4
  371.6 134.8 reduce-scatter.8
where the time goes:
time: 574 us; the launch traced here: 569 us
  waiting for transfers between devices  325 us (57%)
  local copies, waits for them, and re-layouts  102 us (18%)
  blocking collectives  65.3 us (11%)
  matrix products  50.7 us (9%)
  between operations  13.3 us (2%)
  other arithmetic  8.87 us (2%)
    reduce_scatter x2, waiting for transfers between devices, body(): lax.psum_scatter(partial_value.astype(jnp.bfloat16), 'cd', scatter_dimens...  270 us
    all_to_all x2, blocking collectives, body(): lax.all_to_all(rounded, 'cd', split_axis=1, concat_axis=0, tiled=True)  52.6 us
    all_gather x2, waiting for transfers between devices, body(): lax.all_gather(regrouped, 'ab', axis=1, tiled=True)  52.1 us
    rev x2, local copies, waits for them, and re-layouts, swap_rows(): jnp.flip(values.reshape(row_count // 2, 2, -1), axis=1)  51.9 us
    dot_general x2, matrix products, body(): lax.dot_general(lax.all_gather(regrouped, 'ab', axis=1, tiled=True), weig...  44.1 us
    unnamed x13, local copies, waits for them, and re-layouts  20.6 us
    all_to_all x1, blocking collectives, body(): lax.all_to_all(total.reshape(rows_dev, ab_count, tile_area).astype(jnp.bf...  12.7 us
  transfers between devices with their start and end apart: 5, of which 5 were waited for; matrix products, arithmetic and copies ran while one was open for 1% of the time, Pallas kernels for 0%

commit v1 on v0

--- a/solution.py
+++ b/solution.py
@@ -9,18 +9,10 @@
 ITERS = 2
 
 
-def swap_rows(values, diagonal_rows):
-    row_count = values.shape[0]
-    swapped = jnp.flip(values.reshape(row_count // 2, 2, -1), axis=1).reshape(row_count, -1)
-    return jnp.where(diagonal_rows[:, None], values, swapped)
-
-
-def flip_pairs(tiles, diagonal_rows, tile_width):
-    row_count = tiles.shape[0]
-    tile_count = tiles.shape[1]
+def flip_tiles(tiles, tile_width):
+    row_count, tile_count = tiles.shape[:2]
     turned = jnp.swapaxes(tiles.reshape(row_count, tile_count, tile_width, tile_width), 2, 3)
-    turned = turned.reshape(row_count, tile_count * tile_width * tile_width)
-    return swap_rows(turned, diagonal_rows)
+    return turned.reshape(row_count, tile_count * tile_width * tile_width)
 
 
 def body(amplitudes, driver, ladder, block_mask, pair_list, occ_energy, virt_energy):
@@ -52,10 +44,9 @@
     row_energy = jnp.dot(occ_picks, occ_energy, precision=lax.Precision.HIGHEST)
     denominator = col_energy[None, :] - row_energy[:, None]
     local_diagonal = row_pairs // NOCC == row_pairs % NOCC
-    turned_weights = jnp.swapaxes(
-        weights.reshape(out_rows // tile_area, tile_width, tile_width, in_cols), 1, 2
-    )
-    turned_weights = turned_weights.reshape(out_rows, in_cols)
+    row_index = jnp.arange(rows_dev, dtype=jnp.int32)
+    mirror_row = jnp.where(local_diagonal, row_index, row_index ^ 1)
+    row_swap = (mirror_row[:, None] == row_index).astype(jnp.bfloat16)
     state = amplitudes
     for step in range(ITERS):
         rounded = state.astype(jnp.bfloat16)
@@ -66,17 +57,18 @@
             (((1,), (1,)), ((), ())),
             preferred_element_type=jnp.float32,
         )
-        total = lax.psum_scatter(
+        received = lax.psum_scatter(
             partial_value.astype(jnp.bfloat16), "cd", scatter_dimension=0, tiled=True
-        ).astype(jnp.float32)
+        )
+        swapped = jnp.dot(row_swap, received, preferred_element_type=jnp.float32)
         tiles = lax.all_to_all(
-            total.reshape(rows_dev, ab_count, tile_area).astype(jnp.bfloat16),
+            swapped.astype(jnp.bfloat16).reshape(rows_dev, ab_count, tile_area),
             "ab",
             split_axis=1,
             concat_axis=1,
             tiled=True,
-        ).astype(jnp.float32)
-        symmetric = total + flip_pairs(tiles, local_diagonal, tile_width)
+        )
+        symmetric = received.astype(jnp.float32) + flip_tiles(tiles, tile_width).astype(jnp.float32)
         state = (driver + symmetric) / denominator
     return state
 

time: 574 us -> 507 us (0.88)
  local copies, waits for them, and re-layouts: 102 us -> 37.3 us
    reduce_scatter x2 -> x0, waiting for transfers between devices: 270 us -> none  [body(): lax.psum_scatter(partial_value.astype(jnp.bfloat16), 'cd', scatter_dimens...]
    unnamed x4 -> x6, waiting for transfers between devices: 0.07 us -> 269 us
    rev x2 -> x0, local copies, waits for them, and re-layouts: 51.9 us -> none  [swap_rows(): jnp.flip(values.reshape(row_count // 2, 2, -1), axis=1)]
    convert_element_type x2 -> x6, local copies, waits for them, and re-layouts: 2.38 us -> 13.3 us  [body(): flip_tiles(tiles, tile_width).astype(jnp.float32)]
    transpose x4 -> x0, local copies, waits for them, and re-layouts: 9.5 us -> none  [flip_pairs(): jnp.swapaxes(tiles.reshape(row_count, tile_count, tile_width, tile_width)...]
    unnamed x13 -> x11, local copies, waits for them, and re-layouts: 20.6 us -> 16.7 us
where the time goes in v1:
time: 507 us
  waiting for transfers between devices  325 us (64%)
  blocking collectives  65.1 us (13%)
  matrix products  53.8 us (11%)
  local copies, waits for them, and re-layouts  37.3 us (7%)
  between operations  13.3 us (3%)
  other arithmetic  8.42 us (2%)
    unnamed x6, waiting for transfers between devices  269 us
    all_to_all x2, blocking collectives, body(): lax.all_to_all(rounded, 'cd', split_axis=1, concat_axis=0, tiled=True)  52.4 us
    all_gather x2, waiting for transfers between devices, body(): lax.all_gather(regrouped, 'ab', axis=1, tiled=True)  52 us
    dot_general x2, matrix products, body(): lax.dot_general(lax.all_gather(regrouped, 'ab', axis=1, tiled=True), weig...  44.1 us
    unnamed x11, local copies, waits for them, and re-layouts  16.7 us
    convert_element_type x6, local copies, waits for them, and re-layouts, body(): flip_tiles(tiles, tile_width).astype(jnp.float32)  13.3 us
    all_to_all x1, blocking collectives, body(): lax.all_to_all(swapped.astype(jnp.bfloat16).reshape(rows_dev, ab_count, t...  12.7 us
  transfers between devices with their start and end apart: 5, of which 5 were waited for; matrix products, arithmetic and copies ran while one was open for 1% of the time, Pallas kernels for 0%

profile of v1, /device:TPU:0, one launch (start us, length us, event | category | flops | bytes accessed | tf_op | source)
XLA Modules:
  0.0 506.6 jit_solution(11198391696417357768)
XLA Ops:
  6.5 0.0 copy-start
  6.5 0.0 copy-start.2
  6.5 0.0 all-gather.3.cloned.1.call-start
  6.5 1.5 convert_element_type.68
  8.1 0.1 copy.81
  8.1 27.4 %all_to_all.48 = bf16[48,16,512]{2,0,1:T(8,128)(2,1)} all-to-all(bf16[48,16,512]{2,0,1:T(8,128)(2,1)S(1)} %bitcast.62), channel_id=1, replica_groups=mesh['ab'=2,'cd'=16] {'cd'}, dimensions={1} | all-to-all | bytes 1572864 | tf_op jit(solution)/shard_map/all_to_all | solution.py:53
  35.5 0.0 all-gather.3.cloned.1.call-update
  35.6 0.0 reduce-scatter.7.cloned.1.call-start
  35.6 0.0 copy-done.2
  35.6 0.1 copy.52
  35.7 26.5 %all-gather.3.cloned.1.call-done = bf16[768,1024]{1,0:T(8,128)(2,1)} async-done(((bf16[768,512]{1,0:T(8,128)(2,1)}), bf16[768,1024]{1,0:T(8,128)(2,1)}) %all-gather.3.cloned.1.call-update) | async-done | bytes 1572880 | tf_op jit(solution)/shard_map/all_gather | solution.py:55
  62.2 0.0 copy-start.3
  62.2 6.1 %mul.31 = bf16[64,128,8,128]{3,2,1,0:T(8,128)(2,1)} broadcast(bf16[64,8]{1,0:T(8,128)(2,1)S(1)} %copy.52), dimensions={0,2} | broadcast | bytes 16778240 | tf_op jit(solution)/shard_map/mul | solution.py:27
  68.3 0.0 copy-done.3
  68.3 22.4 %fusion = bf16[768,8192]{0,1:T(8,128)(2,1)} fusion(bf16[768,1024]{1,0:T(8,128)(2,1)S(1)} %copy-done.3, bf16[8192,1024]{1,0:T(8,128)(2,1)} %param.9, bf16[1024,8,8,128]{3,2,1,0:T(8,128)(2,1)} %bitcast.55), kind=kOutput, calls=%fused_computation.3 | convolution fusion | flops 12899581952 | bytes 47710208 | tf_op jit(solution)/shard_map/dot_general | solution.py:54
  90.7 16.7 %copy.62 = bf16[768,8192]{1,0:T(8,128)(2,1)} copy(bf16[768,8192]{0,1:T(8,128)(2,1)} %fusion) | data formatting | bytes 25165824
  107.4 0.0 reduce-scatter.7.cloned.1.call-update
  107.4 0.0 copy-start.4
  107.4 0.8 compare_select_fusion
  108.2 134.3 %reduce-scatter.7.cloned.1.call-done = bf16[48,8192]{1,0:T(8,128)(2,1)} async-done(((bf16[768,8192]{1,0:T(8,128)(2,1)}), bf16[48,8192]{1,0:T(8,128)(2,1)}) %reduce-scatter.7.cloned.1.call-update) | async-done | bytes 786448
  242.5 1.5 convolution_convert_fusion.3
  244.0 0.9 copy.80
  244.9 3.5 all-to-all-start.1
  248.5 0.0 all-gather.5.cloned.1.call-start
  248.5 0.1 fusion.10
  248.6 0.0 copy-done.4
  248.6 0.2 convolution_bitcast_fusion
  248.8 0.0 copy-done
  248.8 6.4 %fusion.1 = f32[1,8192]{1,0:T(1,128)S(1)} fusion(s32[8192]{0:T(1024)S(1)} %get-tuple-element.9, s32[8192]{0:T(1024)S(1)} %get-tuple-element.8, f32[128]{0:T(128)S(1)} %copy-done), kind=kOutput, calls=%fused_computation.6 | convolution fusion | flops 17825792 | bytes 98816 | tf_op jit(solution)/shard_map/dot_general | solution.py:39
  255.3 3.5 all-to-all-done.1
  258.7 2.4 reshape.139
  261.1 2.4 copy.56
  263.5 1.9 reshape.137
  265.4 2.5 fusion.7
  267.9 0.1 copy.79
  268.0 25.0 %all_to_all.49 = bf16[48,16,512]{2,0,1:T(8,128)(2,1)} all-to-all(bf16[48,16,512]{2,0,1:T(8,128)(2,1)S(1)} %bitcast.63), channel_id=1, replica_groups=mesh['ab'=2,'cd'=16] {'cd'}, dimensions={1} | all-to-all | bytes 1572864 | tf_op jit(solution)/shard_map/all_to_all | solution.py:53
  292.9 0.0 all-gather.5.cloned.1.call-update
  293.0 0.2 reduce-scatter.9.cloned.1.call-start
  293.2 25.5 %all-gather.5.cloned.1.call-done = bf16[768,1024]{1,0:T(8,128)(2,1)} async-done(((bf16[768,512]{1,0:T(8,128)(2,1)}), bf16[768,1024]{1,0:T(8,128)(2,1)}) %all-gather.5.cloned.1.call-update) | async-done | bytes 1572880 | tf_op jit(solution)/shard_map/all_gather | solution.py:55
  318.7 21.7 %convolution_convert_fusion = bf16[768,8192]{1,0:T(8,128)(2,1)} fusion(bf16[768,1024]{1,0:T(8,128)(2,1)} %all-gather.5.cloned.1.call-done, bf16[8192,1024]{1,0:T(8,128)(2,1)} %param.9, bf16[1024,8,8,128]{3,2,1,0:T(8,128)(2,1)} %bitcast.56), kind=kOutput, calls=%fused_computation.1 | convolution fusion | flops 12899581952 | bytes 47710208 | tf_op jit(solution)/shard_map/dot_general | solution.py:54
  340.4 0.0 reduce-scatter.9.cloned.1.call-update
  340.4 135.1 %reduce-scatter.9.cloned.1.call-done = bf16[48,8192]{1,0:T(8,128)(2,1)} async-done(((bf16[768,8192]{1,0:T(8,128)(2,1)}), bf16[48,8192]{1,0:T(8,128)(2,1)}) %reduce-scatter.9.cloned.1.call-update) | async-done | bytes 786448
  475.5 1.5 convolution_convert_fusion.2
  477.0 0.1 copy.78
  477.1 12.7 %all_to_all.50 = bf16[48,2,4096]{2,0,1:T(8,128)(2,1)S(1)} all-to-all(bf16[48,2,4096]{2,0,1:T(8,128)(2,1)S(1)} %bitcast.65), channel_id=1, replica_groups=mesh['ab'=2,'cd'=16] {'ab'}, dimensions={1} | all-to-all | bytes 1572864 | tf_op jit(solution)/shard_map/all_to_all | solution.py:64
  489.8 2.4 reshape.140
  492.2 2.4 copy.61
  494.5 0.0 copy-start.1
  494.6 1.9 reshape.138
  496.5 3.6 subtract_divide_fusion
  500.1 0.0 copy-done.1
  (1 shorter events, 0.0 us)
Async XLA Ops:
  6.5 242.3 %copy-start = (f32[128]{0:T(128)S(1)}, f32[128]{0:T(128)}, u32[]{:S(2)}) copy-start(f32[128]{0:T(128)} %param.13) | copy-start | bytes 1540
  6.5 29.1 %copy-start.2 = (s32[64,8]{0,1:T(8,128)S(1)}, s32[64,8]{0,1:T(8,128)}, u32[]{:S(2)}) copy-start(s32[64,8]{0,1:T(8,128)} %param.10) | copy-start | bytes 6148
  6.5 55.7 %all-gather.3.cloned.1.call-start = ((), (), s32[]{:S(2)}) async-start(), calls=%async_computation.6 | async-start | bytes 2359296 | tf_op jit(solution)/shard_map/all_gather | solution.py:55
  35.6 206.9 %reduce-scatter.7.cloned.1.call-start = ((), (), s32[]{:S(2)}) async-start(), calls=%async_computation.8 | async-start | bytes 13369344
  62.2 6.1 %copy-start.3 = (bf16[768,1024]{1,0:T(8,128)(2,1)S(1)}, bf16[768,1024]{1,0:T(8,128)(2,1)}, u32[]{:S(2)}) copy-start(bf16[768,1024]{1,0:T(8,128)(2,1)} %all-gather.3.cloned.1.call-done) | copy-start | bytes 4718596
  107.4 141.2 %copy-start.4 = (f32[32]{0:T(128)S(1)}, f32[32]{0:T(128)}, u32[]{:S(2)}) copy-start(f32[32]{0:T(128)} %param.12) | copy-start | bytes 388
  244.9 13.8 %all-to-all-start.1 = ((bf16[48,2,4096]{2,0,1:T(8,128)(2,1)}), bf16[48,2,4096]{2,0,1:T(8,128)(2,1)S(1)}, u32[]{:S(2)}, u32[]{:S(2)}) async-start(bf16[48,2,4096]{2,0,1:T(8,128)(2,1)} %bitcast.53), calls=%async_computation.1 | async-start | bytes 1572864 | tf_op jit(solution)/shard_map/all_to_all | solution.py:64
  248.5 70.2 %all-gather.5.cloned.1.call-start = ((), (), s32[]{:S(2)}) async-start(), calls=%async_computation.7 | async-start | bytes 2359296 | tf_op jit(solution)/shard_map/all_gather | solution.py:55
  293.0 182.5 %reduce-scatter.9.cloned.1.call-start = ((), (), s32[]{:S(2)}) async-start(), calls=%async_computation.9 | async-start | bytes 13369344
  494.5 5.5 %copy-start.1 = (f32[128]{0:T(128)S(1)}, f32[128]{0:T(128)}, u32[]{:S(2)}) copy-start(f32[128]{0:T(128)} %param.13) | copy-start | bytes 1540
Sparse Core Ops, SparseCore 0:
  35.7 26.4 all-gather.2
  107.5 134.9 reduce-scatter.6
  293.1 25.5 all-gather.4
  340.5 134.9 reduce-scatter.8

commit v2 on v1

--- a/solution.py
+++ b/solution.py
@@ -7,12 +7,21 @@
 NOCC = 32
 BLK = 128
 ITERS = 2
+CORES = 2
+CHUNKS = 2
 
 
 def flip_tiles(tiles, tile_width):
     row_count, tile_count = tiles.shape[:2]
     turned = jnp.swapaxes(tiles.reshape(row_count, tile_count, tile_width, tile_width), 2, 3)
     return turned.reshape(row_count, tile_count * tile_width * tile_width)
+
+
+def product(rows, weight):
+    flat = rows.reshape(-1, rows.shape[-1])
+    return lax.dot_general(
+        flat, weight, (((1,), (1,)), ((), ())), preferred_element_type=jnp.float32
+    ).astype(jnp.bfloat16)
 
 
 def body(amplitudes, driver, ladder, block_mask, pair_list, occ_energy, virt_energy):
@@ -47,19 +56,31 @@
     row_index = jnp.arange(rows_dev, dtype=jnp.int32)
     mirror_row = jnp.where(local_diagonal, row_index, row_index ^ 1)
     row_swap = (mirror_row[:, None] == row_index).astype(jnp.bfloat16)
+    cd_count = lax.axis_size("cd")
+    core = cd_index % CORES
+    core_swap = [(index, index ^ 1) for index in range(cd_count)]
+    core_groups = [list(range(start, cd_count, CORES)) for start in range(CORES)]
+    chunk_rows = out_rows // CHUNKS
     state = amplitudes
     for step in range(ITERS):
         rounded = state.astype(jnp.bfloat16)
         regrouped = lax.all_to_all(rounded, "cd", split_axis=1, concat_axis=0, tiled=True)
-        partial_value = lax.dot_general(
-            lax.all_gather(regrouped, "ab", axis=1, tiled=True),
-            weights,
-            (((1,), (1,)), ((), ())),
-            preferred_element_type=jnp.float32,
-        )
-        received = lax.psum_scatter(
-            partial_value.astype(jnp.bfloat16), "cd", scatter_dimension=0, tiled=True
-        )
+        gathered = lax.all_gather(regrouped, "ab", axis=1, tiled=True)
+        by_core = gathered.reshape(cd_count // CORES, CORES, rows_dev, in_cols)
+        other_rows = lax.dynamic_index_in_dim(by_core, 1 - core, 1, keepdims=False)
+        own_rows = lax.dynamic_index_in_dim(by_core, core, 1, keepdims=False)
+        pieces = []
+        for chunk in range(CHUNKS):
+            weight = weights[chunk * chunk_rows : (chunk + 1) * chunk_rows]
+            sent = lax.ppermute(product(other_rows, weight), "cd", core_swap)
+            kept = product(own_rows, weight)
+            both = (sent.astype(jnp.float32) + kept.astype(jnp.float32)).astype(jnp.bfloat16)
+            pieces.append(
+                lax.psum_scatter(
+                    both, "cd", scatter_dimension=0, axis_index_groups=core_groups, tiled=True
+                )
+            )
+        received = jnp.concatenate(pieces, axis=1)
         swapped = jnp.dot(row_swap, received, preferred_element_type=jnp.float32)
         tiles = lax.all_to_all(
             swapped.astype(jnp.bfloat16).reshape(rows_dev, ab_count, tile_area),

time: 507 us -> 519 us (1.024)
  blocking collectives: 65.1 us -> 37.1 us
  matrix products: 53.8 us -> 75.8 us
  waiting for transfers between devices: 325 us -> 306 us
  other arithmetic: 8.42 us -> 22.5 us
  local copies, waits for them, and re-layouts: 37.3 us -> 51.1 us
  starting transfers between devices: 3.84 us -> 12.1 us
    unnamed x6, waiting for transfers between devices: 269 us -> 0.1 us
    reduce_scatter x0 -> x4, waiting for transfers between devices: none -> 249 us  [body(): lax.psum_scatter(both, 'cd', scatter_dimension=0, axis_index_groups=core_...]
    all_to_all x2 -> x1, blocking collectives: 52.4 us -> 24.3 us  [body(): lax.all_to_all(rounded, 'cd', split_axis=1, concat_axis=0, tiled=True)]
    dot_general x2 -> x8, matrix products: 44.1 us -> 68.4 us  [product(): lax.dot_general(flat, weight, (((1,), (1,)), ((), ())), preferred_element...]
    all_gather x2, waiting for transfers between devices: 52 us -> 28 us  [body(): gathered = lax.all_gather(regrouped, 'ab', axis=1, tiled=True)]
    ppermute x0 -> x4, waiting for transfers between devices: none -> 22.4 us  [body(): sent = lax.ppermute(product(other_rows, weight), 'cd', core_swap)]
    mul x0 -> x1, other arithmetic: none -> 14.1 us  [body(): weights * block_mask.astype(jnp.bfloat16)[:, None, :, None]]
    slice x0 -> x1, local copies, waits for them, and re-layouts: none -> 11.5 us  [body(): weight = weights[chunk * chunk_rows:(chunk + 1) * chunk_rows]]
  transfers between devices with their start and end apart: 5 -> 12, of which waited for: 5 -> 12; matrix products, arithmetic and copies ran while one was open for 1% -> 17% of each run, Pallas kernels for 0% -> 0%
where the time goes in v2:
time: 519 us
  waiting for transfers between devices  306 us (59%)
  matrix products  75.8 us (15%)
  local copies, waits for them, and re-layouts  51.1 us (10%)
  blocking collectives  37.1 us (7%)
  other arithmetic  22.5 us (4%)
  between operations  13.7 us (3%)
  starting transfers between devices  12.1 us (2%)
    reduce_scatter x4, waiting for transfers between devices, body(): lax.psum_scatter(both, 'cd', scatter_dimension=0, axis_index_groups=core_...  249 us
    dot_general x8, matrix products, product(): lax.dot_general(flat, weight, (((1,), (1,)), ((), ())), preferred_element...  68.4 us
    all_gather x2, waiting for transfers between devices, body(): gathered = lax.all_gather(regrouped, 'ab', axis=1, tiled=True)  28 us
    all_to_all x1, blocking collectives, body(): lax.all_to_all(rounded, 'cd', split_axis=1, concat_axis=0, tiled=True)  24.3 us
    ppermute x4, waiting for transfers between devices, body(): sent = lax.ppermute(product(other_rows, weight), 'cd', core_swap)  22.4 us
    unnamed x25, local copies, waits for them, and re-layouts  18.6 us
    mul x1, other arithmetic, body(): weights * block_mask.astype(jnp.bfloat16)[:, None, :, None]  14.1 us
    convert_element_type x6, local copies, waits for them, and re-layouts, body(): flip_tiles(tiles, tile_width).astype(jnp.float32)  13.4 us
  transfers between devices with their start and end apart: 12, of which 12 were waited for; matrix products, arithmetic and copies ran while one was open for 17% of the time, Pallas kernels for 0%

profile of v2, /device:TPU:0, one launch (start us, length us, event | category | flops | bytes accessed | tf_op | source)
XLA Modules:
  0.0 518.5 jit_solution(6087048168829518617)
XLA Ops:
  6.5 1.5 convert_element_type.118
  8.0 1.0 copy.83
  9.0 7.4 %all-to-all-start = ((bf16[48,16,512]{2,0,1:T(8,128)(2,1)}), bf16[48,16,512]{2,0,1:T(8,128)(2,1)S(1)}, u32[]{:S(2)}, u32[]{:S(2)}) async-start(bf16[48,16,512]{2,0,1:T(8,128)(2,1)} %bitcast.106), calls=%async_computation | async-start | bytes 1572864 | tf_op jit(solution)/shard_map/all_to_all | solution.py:67
  16.4 0.0 all-gather.3.cloned.1.call-start
  16.5 15.6 %copy.33 = bf16[1024,8,8,128]{3,2,1,0:T(8,128)(2,1)} copy(bf16[1024,8,8,128]{3,1,2,0:T(8,128)(2,1)} %bitcast.109) | data formatting | bytes 33554432
  32.1 0.1 copy.23
  32.2 2.9 all-to-all-done
  35.1 0.9 copy-done.4
  36.0 0.0 reduce-scatter.5.cloned.1.call-start
  36.0 14.1 %bitcast_multiply_fusion = bf16[64,128,8,128]{3,2,1,0:T(8,128)(2,1)} fusion(bf16[64,8]{1,0:T(8,128)(2,1)S(1)} %copy.23, bf16[64,128,8,128]{3,2,1,0:T(8,128)(2,1)} %bitcast.108), kind=kLoop, calls=%fused_computation | loop fusion | flops 8388608 | bytes 33555456 | tf_op jit(solution)/shard_map/mul | solution.py:36
  50.1 11.5 %fusion.86 = (bf16[32,128,8,128]{3,2,1,0:T(8,128)(2,1)}, bf16[32,128,8,128]{3,2,1,0:T(8,128)(2,1)}) fusion(bf16[64,128,8,128]{3,2,1,0:T(8,128)(2,1)} %bitcast_multiply_fusion), kind=kLoop, calls=%fused_computation.114 | loop fusion | bytes 33554432 | tf_op jit(solution)/shard_map/slice | solution.py:74
  61.7 2.4 all-gather.3.cloned.1.call-done
  64.1 1.7 constant_dynamic-slice_fusion.2
  65.8 9.4 %fusion.16 = bf16[384,4096]{1,0:T(8,128)(2,1)S(1)} fusion(bf16[384,1024]{1,0:T(8,128)(2,1)S(1)} %bitcast.140, bf16[512,8,8,128]{3,2,1,0:T(8,128)(2,1)} %bitcast.116), kind=kOutput, calls=%fused_computation.23 | convolution fusion | flops 3222798336 | bytes 12320768 | tf_op jit(solution)/shard_map/dot_general | solution.py:22
  75.2 0.1 collective-permute-start
  75.3 5.6 %collective-permute-done = bf16[384,4096]{1,0:T(8,128)(2,1)S(1)} collective-permute-done((bf16[384,4096]{1,0:T(8,128)(2,1)S(1)}, bf16[384,4096]{1,0:T(8,128)(2,1)S(1)}, u32[]{:S(2)}, u32[]{:S(2)}) %collective-permute-start) | collective-permute-done | bytes 3145760 | tf_op jit(solution)/shard_map/ppermute | solution.py:75
  80.9 5.1 add_convert_fusion.3
  86.0 0.0 reduce-scatter.7.cloned.1.call-start
  86.1 9.2 %fusion.28 = bf16[384,4096]{1,0:T(8,128)(2,1)S(1)} fusion(bf16[384,1024]{1,0:T(8,128)(2,1)S(1)} %bitcast.141, bf16[512,8,8,128]{3,2,1,0:T(8,128)(2,1)} %bitcast.112), kind=kOutput, calls=%fused_computation.27 | convolution fusion | flops 3222798336 | bytes 12320768 | tf_op jit(solution)/shard_map/dot_general | solution.py:22
  95.3 0.2 collective-permute-start.1
  95.5 5.6 %collective-permute-done.1 = bf16[384,4096]{1,0:T(8,128)(2,1)S(1)} collective-permute-done((bf16[384,4096]{1,0:T(8,128)(2,1)S(1)}, bf16[384,4096]{1,0:T(8,128)(2,1)S(1)}, u32[]{:S(2)}, u32[]{:S(2)}) %collective-permute-start.1) | collective-permute-done | bytes 3145760 | tf_op jit(solution)/shard_map/ppermute | solution.py:75
  101.0 10.5 %add_convert_fusion.2 = bf16[384,4096]{1,0:T(8,128)(2,1)} fusion(bf16[384,4096]{1,0:T(8,128)(2,1)S(1)} %collective-permute-done.1, bf16[384,1024]{1,0:T(8,128)(2,1)S(1)} %bitcast.137, bf16[512,8,8,128]{3,2,1,0:T(8,128)(2,1)} %bitcast.113), kind=kOutput, calls=%fused_computation.21 | convolution fusion | flops 3229089792 | bytes 15466496 | tf_op jit(solution)/shard_map/dot_general | solution.py:22
  111.6 0.8 compare_select_fusion
  112.3 48.3 %reduce-scatter.5.cloned.1.call-done = bf16[48,4096]{1,0:T(8,128)(2,1)} async-done(((bf16[384,4096]{1,0:T(8,128)(2,1)}), bf16[48,4096]{1,0:T(8,128)(2,1)}) %reduce-scatter.5.cloned.1.call-update) | async-done | bytes 393232 | tf_op jit(solution)/shard_map/reduce_scatter | solution.py:79
  160.7 1.0 constant_dynamic-update-slice_fusion.1
  161.7 76.1 %reduce-scatter.7.cloned.1.call-done = bf16[48,4096]{1,0:T(8,128)(2,1)} async-done(((bf16[384,4096]{1,0:T(8,128)(2,1)}), bf16[48,4096]{1,0:T(8,128)(2,1)}) %reduce-scatter.7.cloned.1.call-update) | async-done | bytes 393232 | tf_op jit(solution)/shard_map/reduce_scatter | solution.py:79
  237.8 1.0 constant_dynamic-update-slice_fusion
  238.8 0.4 convolution_convert_fusion.1
  239.2 0.9 copy.82
  240.2 3.5 all-to-all-start.1
  243.7 0.2 all-gather.5.cloned.1.call-start
  243.9 0.1 fusion.65
  244.0 0.2 convolution_bitcast_fusion
  244.2 6.4 %fusion.56 = f32[1,8192]{1,0:T(1,128)S(1)} fusion(s32[8192]{0:T(1024)S(1)} %get-tuple-element.15, s32[8192]{0:T(1024)S(1)} %get-tuple-element.14, f32[128]{0:T(128)S(1)} %copy-done), kind=kOutput, calls=%fused_computation.39 | convolution fusion | flops 17825792 | bytes 98816 | tf_op jit(solution)/shard_map/dot_general | solution.py:48
  250.7 3.4 all-to-all-done.1
  254.0 2.4 reshape.175
  256.4 2.4 copy.25
  258.8 1.9 reshape.173
  260.7 2.5 fusion.62
  263.2 0.1 copy.81
  263.3 24.3 %all_to_all.48 = bf16[48,16,512]{2,0,1:T(8,128)(2,1)} all-to-all(bf16[48,16,512]{2,0,1:T(8,128)(2,1)S(1)} %bitcast.127), channel_id=1, replica_groups=mesh['ab'=2,'cd'=16] {'cd'}, dimensions={1} | all-to-all | bytes 1572864 | tf_op jit(solution)/shard_map/all_to_all | solution.py:67
  287.6 0.0 reduce-scatter.9.cloned.1.call-start
  287.6 25.6 %all-gather.5.cloned.1.call-done = bf16[768,1024]{1,0:T(8,128)(2,1)} async-done(((bf16[768,512]{1,0:T(8,128)(2,1)}), bf16[768,1024]{1,0:T(8,128)(2,1)}) %all-gather.5.cloned.1.call-update) | async-done | bytes 1572880 | tf_op jit(solution)/shard_map/all_gather | solution.py:68
  313.3 1.7 constant_dynamic-slice_fusion
  315.0 9.4 %fusion.22 = bf16[384,4096]{1,0:T(8,128)(2,1)S(1)} fusion(bf16[384,1024]{1,0:T(8,128)(2,1)S(1)} %bitcast.138, bf16[512,8,8,128]{3,2,1,0:T(8,128)(2,1)} %bitcast.117), kind=kOutput, calls=%fused_computation.25 | convolution fusion | flops 3222798336 | bytes 12320768 | tf_op jit(solution)/shard_map/dot_general | solution.py:22
  324.4 0.1 collective-permute-start.2
  324.4 5.6 %collective-permute-done.2 = bf16[384,4096]{1,0:T(8,128)(2,1)S(1)} collective-permute-done((bf16[384,4096]{1,0:T(8,128)(2,1)S(1)}, bf16[384,4096]{1,0:T(8,128)(2,1)S(1)}, u32[]{:S(2)}, u32[]{:S(2)}) %collective-permute-start.2) | collective-permute-done | bytes 3145760 | tf_op jit(solution)/shard_map/ppermute | solution.py:75
  330.1 5.1 add_convert_fusion.1
  335.2 0.3 reduce-scatter.11.cloned.1.call-start
  335.5 9.2 %fusion.34 = bf16[384,4096]{1,0:T(8,128)(2,1)S(1)} fusion(bf16[384,1024]{1,0:T(8,128)(2,1)S(1)} %bitcast.139, bf16[512,8,8,128]{3,2,1,0:T(8,128)(2,1)} %bitcast.114), kind=kOutput, calls=%fused_computation.29 | convolution fusion | flops 3222798336 | bytes 12320768 | tf_op jit(solution)/shard_map/dot_general | solution.py:22
  344.7 0.2 collective-permute-start.3
  344.9 5.6 %collective-permute-done.3 = bf16[384,4096]{1,0:T(8,128)(2,1)S(1)} collective-permute-done((bf16[384,4096]{1,0:T(8,128)(2,1)S(1)}, bf16[384,4096]{1,0:T(8,128)(2,1)S(1)}, u32[]{:S(2)}, u32[]{:S(2)}) %collective-permute-start.3) | collective-permute-done | bytes 3145760 | tf_op jit(solution)/shard_map/ppermute | solution.py:75
  350.4 10.5 %add_convert_fusion = bf16[384,4096]{1,0:T(8,128)(2,1)} fusion(bf16[384,4096]{1,0:T(8,128)(2,1)S(1)} %collective-permute-done.3, bf16[384,1024]{1,0:T(8,128)(2,1)S(1)} %bitcast.135, bf16[512,8,8,128]{3,2,1,0:T(8,128)(2,1)} %bitcast.115), kind=kOutput, calls=%fused_computation.19 | convolution fusion | flops 3229089792 | bytes 15466496 | tf_op jit(solution)/shard_map/dot_general | solution.py:22
  361.0 49.2 %reduce-scatter.9.cloned.1.call-done = bf16[48,4096]{1,0:T(8,128)(2,1)} async-done(((bf16[384,4096]{1,0:T(8,128)(2,1)}), bf16[48,4096]{1,0:T(8,128)(2,1)}) %reduce-scatter.9.cloned.1.call-update) | async-done | bytes 393232 | tf_op jit(solution)/shard_map/reduce_scatter | solution.py:79
  410.1 1.0 constant_dynamic-update-slice_fusion.3
  411.2 75.9 %reduce-scatter.11.cloned.1.call-done = bf16[48,4096]{1,0:T(8,128)(2,1)} async-done(((bf16[384,4096]{1,0:T(8,128)(2,1)}), bf16[48,4096]{1,0:T(8,128)(2,1)}) %reduce-scatter.11.cloned.1.call-update) | async-done | bytes 393232 | tf_op jit(solution)/shard_map/reduce_scatter | solution.py:79
  487.0 1.0 constant_dynamic-update-slice_fusion.2
  488.1 0.4 convolution_convert_fusion
  488.5 0.1 copy.80
  488.5 12.8 %all_to_all.49 = bf16[48,2,4096]{2,0,1:T(8,128)(2,1)S(1)} all-to-all(bf16[48,2,4096]{2,0,1:T(8,128)(2,1)S(1)} %bitcast.129), channel_id=1, replica_groups=mesh['ab'=2,'cd'=16] {'ab'}, dimensions={1} | all-to-all | bytes 1572864 | tf_op jit(solution)/shard_map/all_to_all | solution.py:85
  501.4 2.4 reshape.176
  503.8 2.4 copy.28
  506.2 1.9 reshape.174
  508.1 3.6 subtract_divide_fusion
  (30 shorter events, 0.1 us)
Async XLA Ops:
  6.5 237.7 %copy-start = (f32[128]{0:T(128)S(1)}, f32[128]{0:T(128)}, u32[]{:S(2)}) copy-start(f32[128]{0:T(128)} %param.13) | copy-start | bytes 1540
  9.0 26.1 %all-to-all-start = ((bf16[48,16,512]{2,0,1:T(8,128)(2,1)}), bf16[48,16,512]{2,0,1:T(8,128)(2,1)S(1)}, u32[]{:S(2)}, u32[]{:S(2)}) async-start(bf16[48,16,512]{2,0,1:T(8,128)(2,1)} %bitcast.106), calls=%async_computation | async-start | bytes 1572864 | tf_op jit(solution)/shard_map/all_to_all | solution.py:67
  16.4 47.7 %all-gather.3.cloned.1.call-start = ((), (), s32[]{:S(2)}) async-start(), calls=%async_computation.8 | async-start | bytes 2359296 | tf_op jit(solution)/shard_map/all_gather | solution.py:68
  16.4 15.6 %copy-start.5 = (s32[64,8]{0,1:T(8,128)S(1)}, s32[64,8]{0,1:T(8,128)}, u32[]{:S(2)}) copy-start(s32[64,8]{0,1:T(8,128)} %param.10) | copy-start | bytes 6148
  35.1 0.9 copy-start.4
  36.0 124.7 %reduce-scatter.5.cloned.1.call-start = ((), (), s32[]{:S(2)}) async-start(), calls=%async_computation.9 | async-start | bytes 3538944 | tf_op jit(solution)/shard_map/reduce_scatter | solution.py:79
  64.1 16.8 %slice-start = ((s8[8388608]{0:T(1024)(128)(4,1)}), s8[4194304]{0:T(1024)(128)(4,1)S(1)}, s32[]{:S(2)}) async-start(s8[8388608]{0:T(1024)(128)(4,1)} %bitcast.118), calls=%async_computation.14 | async-start | bytes 8388608
  65.8 15.1 %slice-start.1 = ((s8[8388608]{0:T(1024)(128)(4,1)}), s8[4194304]{0:T(1024)(128)(4,1)S(1)}, s32[]{:S(2)}) async-start(s8[8388608]{0:T(1024)(128)(4,1)} %bitcast.118), calls=%async_computation.15 | async-start | bytes 8388608
  75.2 5.7 %collective-permute-start = (bf16[384,4096]{1,0:T(8,128)(2,1)S(1)}, bf16[384,4096]{1,0:T(8,128)(2,1)S(1)}, u32[]{:S(2)}, u32[]{:S(2)}) collective-permute-start(bf16[384,4096]{1,0:T(8,128)(2,1)S(1)} %fusion.16), channel_id=1, source_target_pairs={{0,1},{1,0},{2,3},{3,2},{4,5},{5,4},{6,7},{7,6},{8,9},{9,8},{10,11... | collective-permute-start | bytes 9437192 | tf_op jit(solution)/shard_map/ppermute | solution.py:75
  86.0 151.8 %reduce-scatter.7.cloned.1.call-start = ((), (), s32[]{:S(2)}) async-start(), calls=%async_computation.10 | async-start | bytes 3538944 | tf_op jit(solution)/shard_map/reduce_scatter | solution.py:79
  95.3 5.7 %collective-permute-start.1 = (bf16[384,4096]{1,0:T(8,128)(2,1)S(1)}, bf16[384,4096]{1,0:T(8,128)(2,1)S(1)}, u32[]{:S(2)}, u32[]{:S(2)}) collective-permute-start(bf16[384,4096]{1,0:T(8,128)(2,1)S(1)} %fusion.28), channel_id=1, source_target_pairs={{0,1},{1,0},{2,3},{3,2},{4,5},{5,4},{6,7},{7,6},{8,9},{9,8},{10,11... | collective-permute-start | bytes 9437192 | tf_op jit(solution)/shard_map/ppermute | solution.py:75
  111.5 132.5 %copy-start.6 = (f32[32]{0:T(128)S(1)}, f32[32]{0:T(128)}, u32[]{:S(2)}) copy-start(f32[32]{0:T(128)} %param.12) | copy-start | bytes 388
  238.8 17.6 %copy-start.2 = (bf16[48,8192]{1,0:T(8,128)(2,1)}, bf16[48,8192]{1,0:T(8,128)(2,1)S(1)}, u32[]{:S(2)}) copy-start(bf16[48,8192]{1,0:T(8,128)(2,1)S(1)} %constant_dynamic-update-slice_fusion) | copy-start | bytes 2359300
  240.2 13.9 %all-to-all-start.1 = ((bf16[48,2,4096]{2,0,1:T(8,128)(2,1)}), bf16[48,2,4096]{2,0,1:T(8,128)(2,1)S(1)}, u32[]{:S(2)}, u32[]{:S(2)}) async-start(bf16[48,2,4096]{2,0,1:T(8,128)(2,1)} %bitcast.105), calls=%async_computation.3 | async-start | bytes 1572864 | tf_op jit(solution)/shard_map/all_to_all | solution.py:85
  243.7 69.6 %all-gather.5.cloned.1.call-start = ((), (), s32[]{:S(2)}) async-start(), calls=%async_computation.11 | async-start | bytes 2359296 | tf_op jit(solution)/shard_map/all_gather | solution.py:68
  287.6 122.6 %reduce-scatter.9.cloned.1.call-start = ((), (), s32[]{:S(2)}) async-start(), calls=%async_computation.12 | async-start | bytes 3538944 | tf_op jit(solution)/shard_map/reduce_scatter | solution.py:79
  313.3 16.8 %slice-start.2 = ((s8[8388608]{0:T(1024)(128)(4,1)}), s8[4194304]{0:T(1024)(128)(4,1)S(1)}, s32[]{:S(2)}) async-start(s8[8388608]{0:T(1024)(128)(4,1)} %bitcast.121), calls=%async_computation.16 | async-start | bytes 8388608
  315.0 15.1 %slice-start.3 = ((s8[8388608]{0:T(1024)(128)(4,1)}), s8[4194304]{0:T(1024)(128)(4,1)S(1)}, s32[]{:S(2)}) async-start(s8[8388608]{0:T(1024)(128)(4,1)} %bitcast.121), calls=%async_computation.17 | async-start | bytes 8388608
  324.4 5.7 %collective-permute-start.2 = (bf16[384,4096]{1,0:T(8,128)(2,1)S(1)}, bf16[384,4096]{1,0:T(8,128)(2,1)S(1)}, u32[]{:S(2)}, u32[]{:S(2)}) collective-permute-start(bf16[384,4096]{1,0:T(8,128)(2,1)S(1)} %fusion.22), channel_id=1, source_target_pairs={{0,1},{1,0},{2,3},{3,2},{4,5},{5,4},{6,7},{7,6},{8,9},{9,8},{10,11... | collective-permute-start | bytes 9437192 | tf_op jit(solution)/shard_map/ppermute | solution.py:75
  335.2 151.8 %reduce-scatter.11.cloned.1.call-start = ((), (), s32[]{:S(2)}) async-start(), calls=%async_computation.13 | async-start | bytes 3538944 | tf_op jit(solution)/shard_map/reduce_scatter | solution.py:79
  344.7 5.7 %collective-permute-start.3 = (bf16[384,4096]{1,0:T(8,128)(2,1)S(1)}, bf16[384,4096]{1,0:T(8,128)(2,1)S(1)}, u32[]{:S(2)}, u32[]{:S(2)}) collective-permute-start(bf16[384,4096]{1,0:T(8,128)(2,1)S(1)} %fusion.34), channel_id=1, source_target_pairs={{0,1},{1,0},{2,3},{3,2},{4,5},{5,4},{6,7},{7,6},{8,9},{9,8},{10,11... | collective-permute-start | bytes 9437192 | tf_op jit(solution)/shard_map/ppermute | solution.py:75
  488.1 15.7 %copy-start.3 = (bf16[48,8192]{1,0:T(8,128)(2,1)}, bf16[48,8192]{1,0:T(8,128)(2,1)S(1)}, u32[]{:S(2)}) copy-start(bf16[48,8192]{1,0:T(8,128)(2,1)S(1)} %constant_dynamic-update-slice_fusion.2) | copy-start | bytes 2359300
  503.8 7.9 %copy-start.1 = (f32[128]{0:T(128)S(1)}, f32[128]{0:T(128)}, u32[]{:S(2)}) copy-start(f32[128]{0:T(128)} %param.13) | copy-start | bytes 1540
Sparse Core Ops, SparseCore 0:
  36.1 27.9 all-gather.2
  86.1 74.4 reduce-scatter.4
  164.2 73.4 reduce-scatter.6
  287.7 25.5 all-gather.4
  335.3 74.7 reduce-scatter.8
  413.6 73.4 reduce-scatter.10
